TPU v7x, 32 devices: a whole 2x2x4 slice. The times are simulated.
32 devices in a mesh: groups: 2 (over y), patch: 8 (over z, x), head: 2 (over core).
Axes of the slice: x: 2, y: 2, z: 4, core: 2. Of those that a mesh axis runs over, the one named last changes fastest.
Arguments:
- queries: bfloat16 [2, 256, 1536], P(None, ('groups', 'patch'), 'head'), parts along dimension 1, may hold values from -15 to 15
- stale_pairs: bfloat16 [2, 320, 1536], P(None, ('groups', 'patch'), 'head'), parts along dimension 1, may hold values from -6 to 6
- step_pairs: bfloat16 [2, 2, 320, 1536], P(None, None, ('groups', 'patch'), 'head'), parts along dimension 2, may hold values from -6 to 6
- hidden: bfloat16 [256, 3072], P(('groups', 'patch'), 'head'), parts along dimension 0, may hold values from -3 to 3
- out_weight: bfloat16 [1536, 3072], P('head'), may hold values from -0.15625 to 0.15625
- gate_table: bfloat16 [28, 3072], replicated, may hold values from -4 to 4
- t_index: int32 [4], P('groups'), parts along dimension 0, may hold values from 0 to 27
- text_len: int32 [2], P('groups'), parts along dimension 0, may hold values from 1 to 32
Outputs:
- final_latents: bfloat16 [256, 3072], P(('groups', 'patch', 'head')), parts along dimension 0
There are 2 independent parts, one for each index of `groups`. A program takes and returns all parts, laid end to end along the dimension named above; an argument that names none is the same for every part. Nothing has to cross between parts.
All inputs are finite; a program needn't handle non-finite values.
Results may differ from a plain program's by a relative error of at most 0.0065.
Values may be sent and summed in bfloat16 or wider, within the bound.
A program may use at most 128 MiB of HBM per device.

v0:
```python
import jax
import jax.numpy as jnp
from jax import lax
from jax.sharding import PartitionSpec as P

HDIM = 128


def attend(query_rows, key_rows, value_rows, usable):
    count = query_rows.shape[0]
    total = key_rows.shape[0]
    heads_here = query_rows.shape[1] // HDIM
    qs = query_rows.reshape(count, heads_here, HDIM)
    ks = key_rows.reshape(total, heads_here, HDIM)
    vs = value_rows.reshape(total, heads_here, HDIM)
    scores = jnp.einsum("qhd,khd->hqk", qs, ks, preferred_element_type=jnp.float32) * (
        1.0 / HDIM**0.5
    )
    scores = jnp.where(usable[None, None, :], scores, jnp.float32(-1e30))
    top = jnp.max(scores, axis=2, keepdims=True)
    expo = jnp.exp(scores - top)
    weights = (expo / jnp.sum(expo, axis=2, keepdims=True)).astype(jnp.bfloat16)
    mixed = jnp.einsum("hqk,khd->qhd", weights, vs, preferred_element_type=jnp.float32)
    return mixed.reshape(count, heads_here * HDIM).astype(jnp.bfloat16)


def per_device(queries, stale_pairs, step_pairs, hidden, out_weight, gate_table, t_index, text_len):
    strip_rows = stale_pairs.shape[1]
    lat_rows = queries.shape[1]
    text_rows = strip_rows - lat_rows
    strip_count = lax.axis_size("patch")
    strip_index = lax.axis_index("patch")
    head_index = lax.axis_index("head")
    head_count = lax.axis_size("head")
    total = strip_rows * strip_count
    positions = jnp.arange(total, dtype=jnp.int32)
    within = positions % strip_rows
    holder = positions // strip_rows
    usable = (within < lat_rows) | (holder * text_rows + within - lat_rows < text_len[0])
    old_sets = lax.all_gather(stale_pairs, "patch", axis=1, tiled=True)
    first_sets = lax.all_gather(step_pairs[0], "patch", axis=1, tiled=True)
    remote_sets = (old_sets, first_sets)
    model_width = out_weight.shape[1]
    col_width = model_width // head_count

    def project(section):
        pairs = lax.dynamic_update_slice_in_dim(
            remote_sets[section], step_pairs[section], strip_index * strip_rows, axis=1
        )
        attended = attend(queries[section], pairs[0], pairs[1], usable)
        return jnp.dot(attended, out_weight, preferred_element_type=jnp.float32)

    state = hidden.astype(jnp.float32)
    first_proj = lax.psum_scatter(
        project(0).astype(jnp.bfloat16), "head", scatter_dimension=1, tiled=True
    ).astype(jnp.float32)
    gate_row = gate_table[t_index[0]].astype(jnp.float32)
    state = (
        state
        + lax.dynamic_slice_in_dim(gate_row, head_index * col_width, col_width, 0)[None, :]
        * first_proj
    )
    moved = lax.all_to_all(state, "head", split_axis=0, concat_axis=1, tiled=True)
    last_proj = lax.psum_scatter(project(1), "head", scatter_dimension=0, tiled=True)
    gate_full = gate_table[t_index[1]].astype(jnp.float32)
    return (moved + gate_full[None, :] * last_proj).astype(jnp.bfloat16)


def solution(mesh):
    return jax.shard_map(
        per_device,
        mesh=mesh,
        in_specs=(
            P(None, ("groups", "patch"), "head"),
            P(None, ("groups", "patch"), "head"),
            P(None, None, ("groups", "patch"), "head"),
            P(("groups", "patch"), "head"),
            P("head", None),
            P(),
            P("groups"),
            P("groups"),
        ),
        out_specs=P(("groups", "patch", "head"), None),
        check_vma=False,
    )
```

profile of v0, /device:TPU:0, one launch (start us, length us, event | category | flops | bytes accessed | tf_op | source)
XLA Modules:
  0.0 112.2 jit_solution(2523433137556579357)
XLA Ops:
  6.5 0.0 reduce-scatter.3.cloned.1.call-start
  6.5 0.9 slice_bitcast_fusion
  7.4 33.0 %all-gather = bf16[1,2,160,768]{3,1,0,2:T(2,128)(2,1)S(1)} all-gather(bf16[1,2,20,768]{3,1,0,2:T(2,128)(2,1)S(1)} %slice_bitcast_fusion), channel_id=2, replica_groups=mesh['groups'=2,'patch'=8,'head'=2] {'patch'}, dimensions={2}, use_global_device_ids=true | all-gather | bytes 552960 | tf_op jit(solution)/shard_map/all_gather | solution.py:41
  40.4 31.4 %all_gather.6 = bf16[2,160,768]{2,0,1:T(2,128)(2,1)S(1)} all-gather(bf16[2,20,768]{2,0,1:T(2,128)(2,1)} %param.9), channel_id=1, replica_groups=mesh['groups'=2,'patch'=8,'head'=2] {'patch'}, dimensions={1}, use_global_device_ids=true | all-gather | bytes 552960 | tf_op jit(solution)/shard_map/all_gather | solution.py:40
  71.7 0.8 fusion.33
  72.5 0.1 reshape_squeeze.20
  73.2 1.0 bitcast_dynamic-update-slice_fusion
  74.2 5.2 %slice_reduce_fusion.1 = (bf16[160,768]{1,0:T(8,128)(2,1)S(1)}, bf16[160,768]{1,0:T(8,128)(2,1)S(1)}, bf16[160,768]{1,0:T(8,128)(2,1)S(1)}, bf16[160,768]{1,0:T(8,128)(2,1)S(1)}) fusion(bf16[2,160,768]{2,0,1:T(2,128)(2,1)S(1)} %get-tuple-element.9, bf16[2,160,768]{2,0,1:T(2,128)(2,1)S(1)} %get-tuple-element.10), kind=kLoop, calls=%fused_computation.18 | loop fusion | bytes 1966080 | tf_op jit(solution)/shard_map/slice | solution.py:50
  79.3 0.4 fusion.35
  79.8 0.2 fusion.10
  80.0 0.0 copy-start.1
  80.0 0.0 copy-start
  80.0 3.7 %convolution_convert_fusion = bf16[16,3072]{1,0:T(8,128)(2,1)} fusion(bf16[768,3072]{1,0:T(8,128)(2,1)} %param.12, bf16[6,2,8,128]{3,2,1,0:T(8,128)(2,1)S(1)} %fusion.10), kind=kOutput, calls=%fused_computation.2 | convolution fusion | flops 75546624 | bytes 4841472 | tf_op jit(solution)/shard_map/dot_general | solution.py:51
  83.7 0.0 reduce-scatter.3.cloned.1.call-update
  83.8 0.0 reduce-scatter.5.cloned.1.call-start
  83.8 0.1 reshape_squeeze.23
  83.9 0.4 fusion.36
  84.3 0.2 fusion.11
  84.5 3.7 %fusion.22 = f32[16,3072]{1,0:T(8,128)} fusion(bf16[768,3072]{1,0:T(8,128)(2,1)} %param.12, bf16[6,2,8,128]{3,2,1,0:T(8,128)(2,1)S(1)} %fusion.11), kind=kOutput, calls=%fused_computation.38 | convolution fusion | flops 75497472 | bytes 4939776 | tf_op jit(solution)/shard_map/dot_general | solution.py:51
  88.3 0.0 reduce-scatter.5.cloned.1.call-update
  88.3 0.0 copy-done.1
  88.3 0.6 fusion.34
  92.5 0.8 dynamic-slice_convert_fusion
  93.4 0.8 fusion.29
  94.2 0.0 reduce-scatter.3.cloned.1.call-done
  94.2 0.0 copy-done
  94.2 0.8 add_bitcast_fusion
  95.1 3.8 %all_to_all.19 = f32[2,8,1536]{2,1,0:T(8,128)S(1)} all-to-all(f32[2,8,1536]{2,1,0:T(8,128)S(1)} %add_bitcast_fusion), channel_id=1, replica_groups=mesh['groups'=2,'patch'=8,'head'=2] {'head'}, dimensions={0} | all-to-all | bytes 196608 | tf_op jit(solution)/shard_map/all_to_all | solution.py:63
  98.9 5.0 %reduce-scatter.5.cloned.1.call-done = f32[8,3072]{1,0:T(8,128)} async-done(((f32[16,3072]{1,0:T(8,128)}), f32[8,3072]{1,0:T(8,128)}) %reduce-scatter.5.cloned.1.call-update) | async-done | bytes 98320 | tf_op jit(solution)/shard_map/reduce_scatter | solution.py:64
  103.8 1.5 %add_convert_fusion = bf16[8,3072]{1,0:T(8,128)(2,1)} fusion(f32[8,3072]{1,0:T(8,128)S(1)} %bitcast.74, f32[8,3072]{1,0:T(8,128)} %reduce-scatter.5.cloned.1.call-done, f32[3072]{0:T(1024)S(1)} %bitcast.75), kind=kLoop, calls=%fused_computation.29 | loop fusion | flops 73728 | bytes 258048 | tf_op jit(solution)/shard_map/convert_element_type | solution.py:66
  (1 shorter events, 0.0 us)
Async XLA Ops:
  6.5 87.7 %reduce-scatter.3.cloned.1.call-start = ((), (), s32[]{:S(2)}) async-start(), calls=%async_computation.3 | async-start | bytes 147456 | tf_op jit(solution)/shard_map/reduce_scatter | solution.py:54
  80.0 8.3 %copy-start.1 = (s32[2]{0:T(128)S(1)}, s32[2]{0:T(128)}, u32[]{:S(2)}) copy-start(s32[2]{0:T(128)} %param.14) | copy-start | bytes 28
  80.0 14.2 %copy-start = (bf16[16,1536]{1,0:T(8,128)(2,1)S(1)}, bf16[16,1536]{1,0:T(8,128)(2,1)}, u32[]{:S(2)}) copy-start(bf16[16,1536]{1,0:T(8,128)(2,1)} %param.11) | copy-start | bytes 147460
  83.8 20.1 %reduce-scatter.5.cloned.1.call-start = ((), (), s32[]{:S(2)}) async-start(), calls=%async_computation.4 | async-start | bytes 294912 | tf_op jit(solution)/shard_map/reduce_scatter | solution.py:64
Sparse Core Ops, SparseCore 0:
  83.9 8.8 reduce-scatter.2
  95.1 8.7 reduce-scatter.4
where the time goes:
time: 113 us; the launch traced here: 112 us
  blocking collectives  68.1 us (60%)
  between operations  17.8 us (16%)
  matrix products  8.77 us (8%)
  local copies, waits for them, and re-layouts  8.44 us (7%)
  waiting for transfers between devices  5.03 us (4%)
  other arithmetic  4.01 us (4%)
    all_gather x1, blocking collectives, per_device(): first_sets = lax.all_gather(step_pairs[0], 'patch', axis=1, tiled=True)  33 us
    all_gather x1, blocking collectives, per_device(): old_sets = lax.all_gather(stale_pairs, 'patch', axis=1, tiled=True)  31.4 us
    dot_general x2, matrix products, project(): return jnp.dot(attended, out_weight, preferred_element_type=jnp.float32)  7.5 us
    slice x2, local copies, waits for them, and re-layouts, project(): attended = attend(queries[section], pairs[0], pairs[1], usable)  5.91 us
    reduce_scatter x1, waiting for transfers between devices, per_device(): lax.psum_scatter(project(1), 'head', scatter_dimension=0, tiled=True)  4.98 us
    all_to_all x1, blocking collectives, per_device(): lax.all_to_all(state, 'head', split_axis=0, concat_axis=1, tiled=True)  3.79 us
  transfers between devices with their start and end apart: 2, of which 1 were waited for; matrix products, arithmetic and copies ran while one was open for 7% of the time, Pallas kernels for 0%

commit v1 on v0

--- a/solution.py
+++ b/solution.py
@@ -4,6 +4,28 @@
 from jax.sharding import PartitionSpec as P
 
 HDIM = 128
+
+
+def _point_marks(body, axis_no):
+    t1 = list(body.shape[1:])
+    t1[axis_no] *= body.shape[0]
+    return jnp.moveaxis(body, 0, axis_no).reshape(t1)
+
+
+def put_seats_all_for(sheet, axis_tag):
+    n_axis = lax.axis_size(axis_tag)
+    h_now = sheet[None]
+    for dev in range(n_axis.bit_length() - 1):
+        p_next = 1 << dev
+        u1 = range(n_axis)
+        upper = map(lambda kk: (kk, kk ^ p_next), u1)
+        v1 = list(upper)
+        e_next = lax.ppermute(h_now, axis_name=axis_tag, perm=v1)
+        base_arr = jnp.stack([h_now, e_next])
+        b_next = lax.axis_index(axis_tag)
+        piece_now = b_next >> dev & 1
+        h_now = jnp.where(piece_now == 0, base_arr, base_arr[::-1]).reshape(-1, *sheet.shape)
+    return h_now
 
 
 def attend(query_rows, key_rows, value_rows, usable):
@@ -37,7 +59,8 @@
     within = positions % strip_rows
     holder = positions // strip_rows
     usable = (within < lat_rows) | (holder * text_rows + within - lat_rows < text_len[0])
-    old_sets = lax.all_gather(stale_pairs, "patch", axis=1, tiled=True)
+    found_now = put_seats_all_for(stale_pairs, "patch")
+    old_sets = _point_marks(found_now, 1)
     first_sets = lax.all_gather(step_pairs[0], "patch", axis=1, tiled=True)
     remote_sets = (old_sets, first_sets)
     model_width = out_weight.shape[1]

time: 113 us -> 96.7 us (0.86)
  blocking collectives: 68.1 us -> 35.5 us
  starting transfers between devices: 0.04 us -> 7.31 us
  waiting for transfers between devices: 5.03 us -> 10.3 us
  other arithmetic: 4.01 us -> 6.78 us
    all_gather x1 -> x0, blocking collectives: 31.4 us -> none  [per_device(): old_sets = lax.all_gather(stale_pairs, 'patch', axis=1, tiled=True)]
    ppermute x0 -> x3, starting transfers between devices: none -> 7.26 us  [put_seats_all_for(): e_next = lax.ppermute(h_now, axis_name=axis_tag, perm=v1)]
    ppermute x0 -> x3, waiting for transfers between devices: none -> 2.55 us  [put_seats_all_for(): e_next = lax.ppermute(h_now, axis_name=axis_tag, perm=v1)]
    another operation x0 -> x4, other arithmetic: none -> 2.19 us  [put_seats_all_for(): base_arr = jnp.stack([h_now, e_next])]
    reduce_scatter x1, waiting for transfers between devices: 4.98 us -> 6.42 us  [per_device(): lax.psum_scatter(project(1), 'head', scatter_dimension=0, tiled=True)]
    reduce_scatter x1, waiting for transfers between devices: 0.02 us -> 1.35 us  [per_device(): lax.psum_scatter(project(0).astype(jnp.bfloat16), 'head', scatter_dimensi...]
    all_gather x1, blocking collectives: 33 us -> 31.7 us  [per_device(): first_sets = lax.all_gather(step_pairs[0], 'patch', axis=1, tiled=True)]
  transfers between devices with their start and end apart: 2 -> 5, of which waited for: 1 -> 3; matrix products, arithmetic and copies ran while one was open for 7% -> 10% of each run, Pallas kernels for 0% -> 0%
where the time goes in v1:
time: 96.7 us; the launch traced here: 96 us
  blocking collectives  35.5 us (37%)
  between operations  18.2 us (19%)
  waiting for transfers between devices  10.3 us (11%)
  local copies, waits for them, and re-layouts  9.1 us (9%)
  matrix products  8.76 us (9%)
  starting transfers between devices  7.31 us (8%)
  other arithmetic  6.78 us (7%)
    all_gather x1, blocking collectives, per_device(): first_sets = lax.all_gather(step_pairs[0], 'patch', axis=1, tiled=True)  31.7 us
    dot_general x2, matrix products, project(): return jnp.dot(attended, out_weight, preferred_element_type=jnp.float32)  7.49 us
    ppermute x3, starting transfers between devices, put_seats_all_for(): e_next = lax.ppermute(h_now, axis_name=axis_tag, perm=v1)  7.26 us
    reduce_scatter x1, waiting for transfers between devices, per_device(): lax.psum_scatter(project(1), 'head', scatter_dimension=0, tiled=True)  6.42 us
    slice x2, local copies, waits for them, and re-layouts, project(): attended = attend(queries[section], pairs[0], pairs[1], usable)  5.83 us
    all_to_all x1, blocking collectives, per_device(): lax.all_to_all(state, 'head', split_axis=0, concat_axis=1, tiled=True)  3.79 us
    ppermute x3, waiting for transfers between devices, put_seats_all_for(): e_next = lax.ppermute(h_now, axis_name=axis_tag, perm=v1)  2.55 us
    another operation x4, other arithmetic, put_seats_all_for(): base_arr = jnp.stack([h_now, e_next])  2.19 us
  transfers between devices with their start and end apart: 5, of which 3 were waited for; matrix products, arithmetic and copies ran while one was open for 10% of the time, Pallas kernels for 0%

profile of v1, /device:TPU:0, one launch (start us, length us, event | category | flops | bytes accessed | tf_op | source)
XLA Modules:
  0.0 96.0 jit_solution(15122272511027292682)
XLA Ops:
  6.5 0.0 reduce-scatter.3.cloned.1.call-start
  6.5 3.0 %collective-permute-start = (bf16[1,2,20,768]{3,1,2,0:T(2,128)(2,1)}, bf16[1,2,20,768]{3,1,2,0:T(2,128)(2,1)S(1)}, u32[]{:S(2)}, u32[]{:S(2)}) collective-permute-start(bf16[1,2,20,768]{3,1,2,0:T(2,128)(2,1)} %bitcast.96), channel_id=1, source_target_pairs={{0,2},{2,0},{4,6},{6,4},{8,10},{10,8},{12,14},{14,12},{1,3},{3,1},... | collective-permute-start | bytes 184328 | tf_op jit(solution)/shard_map/ppermute | solution.py:23
  9.5 1.3 %fusion.36 = (s32[1]{0:T(128)}, s32[1]{0:T(128)}) fusion(s32[2]{0:T(128)} %param.14), kind=kLoop, calls=%fused_computation.66 | loop fusion | bytes 16 | tf_op jit(solution)/shard_map/slice | solution.py:88
  12.8 0.8 dynamic-slice_convert_fusion
  13.6 0.9 slice_bitcast_fusion
  15.1 0.0 collective-permute-done
  15.1 1.0 %pad_maximum_fusion.2 = bf16[2,1,2,20,768]{4,2,3,1,0:T(2,128)(2,1)S(1)} fusion(bf16[1,1,2,20,768]{4,2,3,1,0:T(2,128)(2,1)S(1)} %bitcast.98, bf16[1,1,2,20,768]{4,2,3,1,0:T(2,128)(2,1)} %bitcast.97), kind=kLoop, calls=%fused_computation.34 | loop fusion | flops 61440 | bytes 245760 | tf_op jit(solution)/shard_map/stack | solution.py:24
  16.2 0.1 fusion.30
  16.3 1.6 %collective-permute-start.1 = (bf16[2,2,20,768]{3,1,2,0:T(2,128)(2,1)S(1)}, bf16[2,2,20,768]{3,1,2,0:T(2,128)(2,1)S(1)}, u32[]{:S(2)}, u32[]{:S(2)}) collective-permute-start(bf16[2,2,20,768]{3,1,2,0:T(2,128)(2,1)S(1)} %get-tuple-element.12), channel_id=1, source_target_pairs={{0,4},{2,6},{4,0},{6,2},{8,12},{10,14},{12,8},{14,10},{1,5},{3,7},... | collective-permute-start | bytes 368648 | tf_op jit(solution)/shard_map/ppermute | solution.py:23
  17.9 0.8 fusion.35
  18.7 2.5 %collective-permute-done.1 = bf16[2,2,20,768]{3,1,2,0:T(2,128)(2,1)S(1)} collective-permute-done((bf16[2,2,20,768]{3,1,2,0:T(2,128)(2,1)S(1)}, bf16[2,2,20,768]{3,1,2,0:T(2,128)(2,1)S(1)}, u32[]{:S(2)}, u32[]{:S(2)}) %collective-permute-start.1) | collective-permute-done | bytes 122912 | tf_op jit(solution)/shard_map/ppermute | solution.py:23
  21.2 0.3 pad_maximum_fusion.1
  21.6 0.2 broadcast_select_fusion.1
  21.8 2.7 %collective-permute-start.2 = (bf16[4,2,20,768]{3,1,2,0:T(2,128)(2,1)S(1)}, bf16[4,2,20,768]{3,1,2,0:T(2,128)(2,1)S(1)}, u32[]{:S(2)}, u32[]{:S(2)}) collective-permute-start(bf16[4,2,20,768]{3,1,2,0:T(2,128)(2,1)S(1)} %bitcast.91), channel_id=1, source_target_pairs={{0,8},{2,10},{4,12},{6,14},{8,0},{10,2},{12,4},{14,6},{1,9},{3,11}... | collective-permute-start | bytes 737288 | tf_op jit(solution)/shard_map/ppermute | solution.py:23
  25.9 0.1 reshape_squeeze.23
  25.9 0.1 reshape_squeeze.20
  26.7 0.8 fusion.31
  27.5 31.7 %all-gather = bf16[1,2,160,768]{3,1,0,2:T(2,128)(2,1)S(1)} all-gather(bf16[1,2,20,768]{3,1,0,2:T(2,128)(2,1)S(1)} %slice_bitcast_fusion), channel_id=2, replica_groups=mesh['groups'=2,'patch'=8,'head'=2] {'patch'}, dimensions={2}, use_global_device_ids=true | all-gather | bytes 552960 | tf_op jit(solution)/shard_map/all_gather | solution.py:64
  59.2 0.0 collective-permute-done.2
  59.2 0.7 pad_maximum_fusion
  59.9 0.4 broadcast_select_fusion
  60.3 1.0 %bitcast_dynamic-update-slice_fusion = (bf16[2,160,768]{2,0,1:T(2,128)(2,1)S(1)}, bf16[2,160,768]{2,0,1:T(2,128)(2,1)S(1)}) fusion(bf16[2,160,768]{2,0,1:T(2,128)(2,1)S(1)} %bitcast.89, s32[]{:T(128)S(6)} %select_n.80, bf16[2,2,20,768]{3,1,2,0:T(2,128)(2,1)} %param.10, bf16[2,160,768]{2,0,1:T(2,128)(2,1)S(1)} %bitcast.90), kind=kLoop, calls=%fused_computation.39 | loop fusion | bytes 245764 | tf_op jit(solution)/shard_map/dynamic_update_slice | solution.py:70
  61.3 5.1 %slice_reduce_fusion.1 = (bf16[160,768]{1,0:T(8,128)(2,1)S(1)}, bf16[160,768]{1,0:T(8,128)(2,1)S(1)}, bf16[160,768]{1,0:T(8,128)(2,1)S(1)}, bf16[160,768]{1,0:T(8,128)(2,1)S(1)}) fusion(bf16[2,160,768]{2,0,1:T(2,128)(2,1)S(1)} %get-tuple-element.9, bf16[2,160,768]{2,0,1:T(2,128)(2,1)S(1)} %get-tuple-element.10), kind=kLoop, calls=%fused_computation.19 | loop fusion | bytes 1966080 | tf_op jit(solution)/shard_map/slice | solution.py:73
  66.4 0.4 fusion.37
  66.8 0.2 fusion.10
  67.0 0.0 copy-start
  67.0 3.7 %convolution_convert_fusion = bf16[16,3072]{1,0:T(8,128)(2,1)} fusion(bf16[768,3072]{1,0:T(8,128)(2,1)} %param.12, bf16[6,2,8,128]{3,2,1,0:T(8,128)(2,1)S(1)} %fusion.10), kind=kOutput, calls=%fused_computation.2 | convolution fusion | flops 75546624 | bytes 4841472 | tf_op jit(solution)/shard_map/dot_general | solution.py:74
  70.7 0.0 reduce-scatter.3.cloned.1.call-update
  70.8 0.0 reduce-scatter.5.cloned.1.call-start
  70.8 0.4 fusion.38
  71.2 0.2 fusion.11
  71.4 3.8 %fusion.22 = f32[16,3072]{1,0:T(8,128)} fusion(bf16[768,3072]{1,0:T(8,128)(2,1)} %param.12, bf16[6,2,8,128]{3,2,1,0:T(8,128)(2,1)S(1)} %fusion.11), kind=kOutput, calls=%fused_computation.44 | convolution fusion | flops 75497472 | bytes 4939776 | tf_op jit(solution)/shard_map/dot_general | solution.py:74
  75.2 0.0 reduce-scatter.5.cloned.1.call-update
  75.2 1.4 %reduce-scatter.3.cloned.1.call-done = bf16[16,1536]{1,0:T(8,128)(2,1)} async-done(((bf16[16,3072]{1,0:T(8,128)(2,1)}), bf16[16,1536]{1,0:T(8,128)(2,1)}) %reduce-scatter.3.cloned.1.call-update) | async-done | bytes 49168 | tf_op jit(solution)/shard_map/reduce_scatter | solution.py:77
  76.6 0.0 copy-done
  76.6 0.8 add_bitcast_fusion
  77.4 3.8 %all_to_all.19 = f32[2,8,1536]{2,1,0:T(8,128)S(1)} all-to-all(f32[2,8,1536]{2,1,0:T(8,128)S(1)} %add_bitcast_fusion), channel_id=1, replica_groups=mesh['groups'=2,'patch'=8,'head'=2] {'head'}, dimensions={0} | all-to-all | bytes 196608 | tf_op jit(solution)/shard_map/all_to_all | solution.py:86
  81.2 6.4 %reduce-scatter.5.cloned.1.call-done = f32[8,3072]{1,0:T(8,128)} async-done(((f32[16,3072]{1,0:T(8,128)}), f32[8,3072]{1,0:T(8,128)}) %reduce-scatter.5.cloned.1.call-update) | async-done | bytes 98320 | tf_op jit(solution)/shard_map/reduce_scatter | solution.py:87
  87.6 1.5 %add_convert_fusion = bf16[8,3072]{1,0:T(8,128)(2,1)} fusion(f32[8,3072]{1,0:T(8,128)S(1)} %bitcast.93, f32[8,3072]{1,0:T(8,128)} %reduce-scatter.5.cloned.1.call-done, f32[3072]{0:T(1024)S(1)} %bitcast.99), kind=kLoop, calls=%fused_computation.35 | loop fusion | flops 73728 | bytes 258048 | tf_op jit(solution)/shard_map/convert_element_type | solution.py:89
  (1 shorter events, 0.0 us)
Async XLA Ops:
  6.5 70.0 %reduce-scatter.3.cloned.1.call-start = ((), (), s32[]{:S(2)}) async-start(), calls=%async_computation.3 | async-start | bytes 147456 | tf_op jit(solution)/shard_map/reduce_scatter | solution.py:77
  6.5 8.6 %collective-permute-start = (bf16[1,2,20,768]{3,1,2,0:T(2,128)(2,1)}, bf16[1,2,20,768]{3,1,2,0:T(2,128)(2,1)S(1)}, u32[]{:S(2)}, u32[]{:S(2)}) collective-permute-start(bf16[1,2,20,768]{3,1,2,0:T(2,128)(2,1)} %bitcast.96), channel_id=1, source_target_pairs={{0,2},{2,0},{4,6},{6,4},{8,10},{10,8},{12,14},{14,12},{1,3},{3,1},... | collective-permute-start | bytes 184328 | tf_op jit(solution)/shard_map/ppermute | solution.py:23
  16.3 4.9 %collective-permute-start.1 = (bf16[2,2,20,768]{3,1,2,0:T(2,128)(2,1)S(1)}, bf16[2,2,20,768]{3,1,2,0:T(2,128)(2,1)S(1)}, u32[]{:S(2)}, u32[]{:S(2)}) collective-permute-start(bf16[2,2,20,768]{3,1,2,0:T(2,128)(2,1)S(1)} %get-tuple-element.12), channel_id=1, source_target_pairs={{0,4},{2,6},{4,0},{6,2},{8,12},{10,14},{12,8},{14,10},{1,5},{3,7},... | collective-permute-start | bytes 368648 | tf_op jit(solution)/shard_map/ppermute | solution.py:23
  21.8 37.4 %collective-permute-start.2 = (bf16[4,2,20,768]{3,1,2,0:T(2,128)(2,1)S(1)}, bf16[4,2,20,768]{3,1,2,0:T(2,128)(2,1)S(1)}, u32[]{:S(2)}, u32[]{:S(2)}) collective-permute-start(bf16[4,2,20,768]{3,1,2,0:T(2,128)(2,1)S(1)} %bitcast.91), channel_id=1, source_target_pairs={{0,8},{2,10},{4,12},{6,14},{8,0},{10,2},{12,4},{14,6},{1,9},{3,11}... | collective-permute-start | bytes 737288 | tf_op jit(solution)/shard_map/ppermute | solution.py:23
  67.0 9.6 %copy-start = (bf16[16,1536]{1,0:T(8,128)(2,1)S(1)}, bf16[16,1536]{1,0:T(8,128)(2,1)}, u32[]{:S(2)}) copy-start(bf16[16,1536]{1,0:T(8,128)(2,1)} %param.11) | copy-start | bytes 147460
  70.8 16.9 %reduce-scatter.5.cloned.1.call-start = ((), (), s32[]{:S(2)}) async-start(), calls=%async_computation.4 | async-start | bytes 294912 | tf_op jit(solution)/shard_map/reduce_scatter | solution.py:87
Sparse Core Ops, SparseCore 0:
  70.9 5.6 reduce-scatter.2
  78.8 8.7 reduce-scatter.4
